TPU v7x, 256 devices: a whole 4x4x8 slice. The times are simulated.
256 devices in a mesh: expert: 32 (over z, y_lo, core), blk: 8 (over x, y_hi).
Axes of the slice: x: 4, y: 4 (y_hi: 2, y_lo: 2; y = y_hi * 2 + y_lo), z: 8, core: 2. Of those that a mesh axis runs over, the one named last changes fastest.
Arguments:
- tokens: bfloat16 [16384, 7168], P(('expert', 'blk')), may hold values from -6 to 6
- expert_ids: int32 [16384, 8], P(('expert', 'blk')), may hold values from 0 to 255, all different within a row; in each aligned block of 64 rows (0 to 63, 64 to 127, ...) at most 4 rows name the same one
- gate_weights: bfloat16 [16384, 8], P(('expert', 'blk')), may hold values from 0.099609375 to 1
- w_gate: bfloat16 [32, 7168, 2048], P('expert', None, 'blk'), may hold values from -0.0625 to 0.0625
- w_up: bfloat16 [32, 7168, 2048], P('expert', None, 'blk'), may hold values from -0.0625 to 0.0625
- w_down: bfloat16 [32, 2048, 7168], P('expert', None, 'blk'), may hold values from -0.125 to 0.125
Outputs:
- mixed_out: bfloat16 [16384, 7168], P(('expert', 'blk'))
Inputs may be any that keep to these rules, and one draw needn't show every extreme that they name: `expert_ids`: each row names 8 different experts; among the 64 rows of one device no expert is named more than 4 times, a bound that some block reaches.
All inputs are finite; a program needn't handle non-finite values.
Results may differ from a plain program's by a relative error of at most 0.0057.
Values may be sent and summed in bfloat16 or wider, within the bound.
A program may use at most 64 MiB of HBM per device.

v0:
```python
import jax
import jax.numpy as jnp
from jax import lax
from jax.sharding import PartitionSpec as P

CAP = 4


def slot_tables(id_rows, gate_rows, experts, capacity):
    labels = jnp.arange(experts, dtype=jnp.int32)
    matches = id_rows[:, :, None] == labels[None, None, :]
    chosen = jnp.any(matches, axis=1)
    weights = jnp.sum(jnp.where(matches, gate_rows.astype(jnp.float32)[:, :, None], 0.0), axis=1)
    counts = chosen.astype(jnp.int32)
    before = jnp.cumsum(counts, axis=0) - counts
    places = jnp.arange(capacity, dtype=jnp.int32)
    selected = chosen[:, :, None] & (before[:, :, None] == places[None, None, :])
    selector = selected.astype(jnp.bfloat16)
    weighting = jnp.where(selected, weights[:, :, None], 0.0).astype(jnp.bfloat16)
    return (selector, weighting)


def hidden_units(row_block, gate_mat, up_mat):
    gate_part = jnp.dot(row_block, gate_mat, preferred_element_type=jnp.float32)
    up_part = jnp.dot(row_block, up_mat, preferred_element_type=jnp.float32)
    return (jax.nn.silu(gate_part) * up_part).astype(jnp.bfloat16)


def on_device(tokens, expert_ids, gate_weights, w_gate, w_up, w_down):
    gate_mat = w_gate[0]
    up_mat = w_up[0]
    down_mat = w_down[0]
    experts = lax.axis_size("expert")
    blocks = lax.axis_size("blk")
    tok_dev = tokens.shape[0]
    width = tokens.shape[1]
    selector, weighting = slot_tables(expert_ids, gate_weights, experts, CAP)
    outgoing = jnp.einsum(
        "tec,td->ecd", selector, tokens, preferred_element_type=jnp.float32
    ).astype(jnp.bfloat16)
    received = lax.all_to_all(outgoing, "expert", split_axis=0, concat_axis=0, tiled=True)
    mine = received.reshape(experts * CAP, width)
    row_block = lax.all_gather(mine, "blk", axis=0, tiled=True)
    hidden = hidden_units(row_block, gate_mat, up_mat)
    hidden_all = lax.all_gather(hidden, "blk", axis=1, tiled=True)
    slices = jnp.dot(hidden_all, down_mat, preferred_element_type=jnp.float32).astype(jnp.bfloat16)
    slices = slices.reshape(blocks, experts, CAP, -1).transpose(1, 0, 2, 3)
    slices = slices.reshape(experts, blocks * CAP, -1)
    weighting_all = lax.all_gather(
        weighting.reshape(tok_dev, experts * CAP), "blk", axis=0, tiled=True
    ).reshape(blocks, tok_dev, experts, CAP)
    returned = lax.all_to_all(slices, "expert", split_axis=0, concat_axis=0, tiled=True)
    returned = returned.reshape(experts, blocks, CAP, -1)
    partial_out = jnp.einsum(
        "btec,ebcd->btd", weighting_all, returned, preferred_element_type=jnp.float32
    ).astype(jnp.bfloat16)
    partial_out = partial_out.reshape(blocks * tok_dev, -1)
    return lax.all_to_all(partial_out, "blk", split_axis=0, concat_axis=1, tiled=True)


def solution(mesh):
    return jax.shard_map(
        on_device,
        mesh=mesh,
        in_specs=(
            P(("expert", "blk"), None),
            P(("expert", "blk"), None),
            P(("expert", "blk"), None),
            P("expert", None, "blk"),
            P("expert", None, "blk"),
            P("expert", None, "blk"),
        ),
        out_specs=P(("expert", "blk"), None),
        check_vma=False,
    )
```

profile of v0, /device:TPU:8, one launch (start us, length us, event | category | flops | bytes accessed | tf_op | source)
XLA Modules:
  0.0 427.2 jit_solution(4727964634798736242)
XLA Ops:
  6.5 0.0 copy-start
  6.5 0.0 all-gather.3.cloned.1.call-start
  6.5 0.8 fusion.17
  7.3 0.1 copy.44
  7.4 0.1 reduce_window_sum.11
  7.6 0.1 copy.45
  7.7 0.1 copy-done
  7.7 0.6 convolution_convert_fusion
  8.4 1.4 copy.51
  9.8 55.6 %all_to_all.26 = bf16[32,4,7168]{2,1,0:T(4,128)(2,1)S(1)} all-to-all(bf16[32,4,7168]{2,1,0:T(4,128)(2,1)S(1)} %copy.51), channel_id=1, replica_groups=mesh['expert'=32,'blk'=8] {'expert'}, dimensions={0} | all-to-all | bytes 3670016 | tf_op jit(solution)/shard_map/all_to_all | solution.py:41
  65.4 1.4 reshape.42
  66.9 0.0 all-gather.3.cloned.1.call-update
  66.9 0.2 all-gather.5.cloned.1.call-start
  67.1 166.8 %all-gather.3.cloned.1.call-done = bf16[1024,7168]{1,0:T(8,128)(2,1)} async-done(((bf16[128,7168]{1,0:T(8,128)(2,1)}), bf16[1024,7168]{1,0:T(8,128)(2,1)}) %all-gather.3.cloned.1.call-update) | async-done | bytes 14680080 | tf_op jit(solution)/shard_map/all_gather | solution.py:43
  233.9 0.0 copy-start.3
  233.9 0.0 copy-start.4
  233.9 8.8 %fusion.4 = f32[1024,256]{1,0:T(8,128)S(1)} fusion(bf16[1024,7168]{1,0:T(8,128)(2,1)} %all-gather.3.cloned.1.call-done, bf16[1,7168,256]{2,1,0:T(8,128)(2,1)} %param.9), kind=kOutput, calls=%fused_computation.5 | convolution fusion | flops 3758096384 | bytes 19398656 | tf_op jit(solution)/shard_map/dot_general | solution.py:24
  242.7 1.5 copy-done.3
  244.3 1.0 copy-done.4
  245.3 4.8 %fusion.12 = bf16[1024,256]{1,0:T(8,128)(2,1)} fusion(bf16[1024,7168]{1,0:T(8,128)(2,1)S(1)} %copy-done.3, bf16[1,7168,256]{2,1,0:T(8,128)(2,1)S(1)} %copy-done.4, f32[1024,256]{1,0:T(8,128)S(1)} %fusion.4), kind=kOutput, calls=%fused_computation.10 | convolution fusion | flops 3759669248 | bytes 19922944 | tf_op jit(solution)/shard_map/dot_general | solution.py:25
  250.1 0.0 all-gather.5.cloned.1.call-update
  250.1 80.3 %all-gather.5.cloned.1.call-done = bf16[1024,2048]{1,0:T(8,128)(2,1)} async-done(((bf16[1024,256]{1,0:T(8,128)(2,1)}), bf16[1024,2048]{1,0:T(8,128)(2,1)}) %all-gather.5.cloned.1.call-update) | async-done | bytes 4194320 | tf_op jit(solution)/shard_map/all_gather | solution.py:45
  330.4 9.1 %fusion.6 = bf16[1024,896]{1,0:T(8,128)(2,1)} fusion(bf16[1024,2048]{1,0:T(8,128)(2,1)} %all-gather.5.cloned.1.call-done, bf16[1,2048,896]{2,1,0:T(8,128)(2,1)} %param.11), kind=kOutput, calls=%fused_computation.8 | convolution fusion | flops 3759013888 | bytes 9699328 | tf_op jit(solution)/shard_map/dot_general | solution.py:46
  339.5 3.1 reshape.43
  342.6 0.3 copy.52
  342.9 0.0 copy-start.2
  342.9 0.0 copy-start.1
  342.9 1.8 copy.53
  344.8 8.6 %all-to-all-start.1 = ((bf16[32,32,896]{2,1,0:T(8,128)(2,1)}), bf16[32,32,896]{2,1,0:T(8,128)(2,1)S(1)}, u32[]{:S(2)}, u32[]{:S(2)}) async-start(bf16[32,32,896]{2,1,0:T(8,128)(2,1)} %copy.53), calls=%async_computation.1 | async-start | bytes 3670016 | tf_op jit(solution)/shard_map/all_to_all | solution.py:52
  353.4 0.1 copy.46
  353.5 0.1 copy.47
  353.6 0.0 copy-done.2
  353.6 0.0 copy-done.1
  353.7 0.1 copy.48
  353.8 0.1 eq.43
  353.9 34.7 %all_gather.9 = bf16[512,128]{1,0:T(8,128)(2,1)S(1)} all-gather(bf16[64,128]{1,0:T(8,128)(2,1)S(1)} %select_convert_fusion), channel_id=1, replica_groups=mesh['expert'=32,'blk'=8] {'blk'}, dimensions={0}, use_global_device_ids=true | all-gather | bytes 147456 | tf_op jit(solution)/shard_map/all_gather | solution.py:49
  388.6 0.1 copy.49
  388.7 0.2 reshape.41
  388.9 9.2 %all-to-all-done.1 = bf16[32,32,896]{2,1,0:T(8,128)(2,1)S(1)} async-done(((bf16[32,32,896]{2,1,0:T(8,128)(2,1)}), bf16[32,32,896]{2,1,0:T(8,128)(2,1)S(1)}, u32[]{:S(2)}, u32[]{:S(2)}) %all-to-all-start.1) | async-done | bytes 1835040 | tf_op jit(solution)/shard_map/all_to_all | solution.py:52
  398.1 0.6 copy.54
  398.6 0.5 bitcast_convert_fusion
  399.1 20.2 %all_to_all.27 = bf16[8,64,896]{2,1,0:T(8,128)(2,1)S(1)} all-to-all(bf16[8,64,896]{2,1,0:T(8,128)(2,1)S(1)} %bitcast_convert_fusion), channel_id=1, replica_groups=mesh['expert'=32,'blk'=8] {'blk'}, dimensions={0} | all-to-all | bytes 1835008 | tf_op jit(solution)/shard_map/all_to_all | solution.py:58
  419.3 1.1 copy.58
  (10 shorter events, 0.2 us)
Async XLA Ops:
  6.5 1.2 copy-start
  6.5 227.3 %all-gather.3.cloned.1.call-start = ((), (), s32[]{:S(2)}) async-start(), calls=%async_computation.3 | async-start | bytes 16515072 | tf_op jit(solution)/shard_map/all_gather | solution.py:43
  66.9 263.5 %all-gather.5.cloned.1.call-start = ((), (), s32[]{:S(2)}) async-start(), calls=%async_computation.4 | async-start | bytes 4718592 | tf_op jit(solution)/shard_map/all_gather | solution.py:45
  233.9 10.4 %copy-start.3 = (bf16[1024,7168]{1,0:T(8,128)(2,1)S(1)}, bf16[1024,7168]{1,0:T(8,128)(2,1)}, u32[]{:S(2)}) copy-start(bf16[1024,7168]{1,0:T(8,128)(2,1)} %all-gather.3.cloned.1.call-done) | copy-start | bytes 44040196
  233.9 11.4 %copy-start.4 = (bf16[1,7168,256]{2,1,0:T(8,128)(2,1)S(1)}, bf16[1,7168,256]{2,1,0:T(8,128)(2,1)}, u32[]{:S(2)}) copy-start(bf16[1,7168,256]{2,1,0:T(8,128)(2,1)} %param.10) | copy-start | bytes 11010052
  342.9 10.7 %copy-start.2 = (bf16[64,8]{0,1:T(8,128)(2,1)S(1)}, bf16[64,8]{0,1:T(8,128)(2,1)}, u32[]{:S(2)}) copy-start(bf16[64,8]{0,1:T(8,128)(2,1)} %param.8) | copy-start | bytes 3076
  342.9 10.7 %copy-start.1 = (s32[64,8]{0,1:T(8,128)S(1)}, s32[64,8]{0,1:T(8,128)}, u32[]{:S(2)}) copy-start(s32[64,8]{0,1:T(8,128)} %param.7) | copy-start | bytes 6148
  344.8 53.3 %all-to-all-start.1 = ((bf16[32,32,896]{2,1,0:T(8,128)(2,1)}), bf16[32,32,896]{2,1,0:T(8,128)(2,1)S(1)}, u32[]{:S(2)}, u32[]{:S(2)}) async-start(bf16[32,32,896]{2,1,0:T(8,128)(2,1)} %copy.53), calls=%async_computation.1 | async-start | bytes 3670016 | tf_op jit(solution)/shard_map/all_to_all | solution.py:52
Sparse Core Ops, SparseCore 0:
  67.0 166.8 all-gather.2
  250.2 80.1 all-gather.4
where the time goes:
time: 427 us
  waiting for transfers between devices  256 us (60%)
  blocking collectives  110 us (26%)
  matrix products  23.8 us (6%)
  between operations  13.6 us (3%)
  local copies, waits for them, and re-layouts  13.3 us (3%)
  starting transfers between devices  8.85 us (2%)
    all_gather x1, waiting for transfers between devices, on_device(): row_block = lax.all_gather(mine, 'blk', axis=0, tiled=True)  167 us
    all_gather x1, waiting for transfers between devices, on_device(): hidden_all = lax.all_gather(hidden, 'blk', axis=1, tiled=True)  80.3 us
    all_to_all x1, blocking collectives, on_device(): lax.all_to_all(outgoing, 'expert', split_axis=0, concat_axis=0, tiled=True)  55.6 us
    all_gather x1, blocking collectives, on_device(): lax.all_gather(weighting.reshape(tok_dev, experts * CAP), 'blk', axis=0,...  34.7 us
    all_to_all x1, blocking collectives, on_device(): lax.all_to_all(partial_out, 'blk', split_axis=0, concat_axis=1, tiled=True)  20.2 us
    all_to_all x1, waiting for transfers between devices, on_device(): lax.all_to_all(slices, 'expert', split_axis=0, concat_axis=0, tiled=True)  9.15 us
    dot_general x1, matrix products, on_device(): jnp.dot(hidden_all, down_mat, preferred_element_type=jnp.float32)  9.07 us
    dot_general x1, matrix products, hidden_units(): gate_part = jnp.dot(row_block, gate_mat, preferred_element_type=jnp.float32)  8.83 us
  transfers between devices with their start and end apart: 3, of which 3 were waited for; matrix products, arithmetic and copies ran while one was open for 0% of the time, Pallas kernels for 0%

commit v1 on v0

--- a/solution.py
+++ b/solution.py
@@ -40,7 +40,9 @@
     ).astype(jnp.bfloat16)
     received = lax.all_to_all(outgoing, "expert", split_axis=0, concat_axis=0, tiled=True)
     mine = received.reshape(experts * CAP, width)
-    row_block = lax.all_gather(mine, "blk", axis=0, tiled=True)
+    row_block = jnp.concatenate(
+        lax.all_to_all(jnp.stack([mine] * lax.axis_size("blk")), "blk", 0, 0), axis=0
+    )
     hidden = hidden_units(row_block, gate_mat, up_mat)
     hidden_all = lax.all_gather(hidden, "blk", axis=1, tiled=True)
     slices = jnp.dot(hidden_all, down_mat, preferred_element_type=jnp.float32).astype(jnp.bfloat16)

time: 427 us -> 423 us (level)
  blocking collectives: 110 us -> 279 us
  waiting for transfers between devices: 256 us -> 87.2 us
  matrix products: 23.8 us -> 18.9 us
    all_to_all x0 -> x1, blocking collectives: none -> 169 us  [on_device(): lax.all_to_all(jnp.stack([mine] * lax.axis_size('blk')), 'blk', 0, 0)]
    all_gather x1 -> x0, waiting for transfers between devices: 167 us -> none  [on_device(): row_block = lax.all_gather(mine, 'blk', axis=0, tiled=True)]
    another operation x0 -> x2, local copies, waits for them, and re-layouts: none -> 5.18 us  [on_device(): jnp.stack([mine] * lax.axis_size('blk'))]
    dot_general x1, matrix products: 8.83 us -> 3.94 us  [hidden_units(): gate_part = jnp.dot(row_block, gate_mat, preferred_element_type=jnp.float32)]
  transfers between devices with their start and end apart: 3 -> 2, of which waited for: 3 -> 2; matrix products, arithmetic and copies ran while one was open for 0% -> 0% of each run, Pallas kernels for 0% -> 0%
where the time goes in v1:
time: 423 us
  blocking collectives  279 us (66%)
  waiting for transfers between devices  87.2 us (21%)
  matrix products  18.9 us (4%)
  local copies, waits for them, and re-layouts  14.4 us (3%)
  between operations  13.6 us (3%)
  starting transfers between devices  8.63 us (2%)
    all_to_all x1, blocking collectives, on_device(): lax.all_to_all(jnp.stack([mine] * lax.axis_size('blk')), 'blk', 0, 0)  169 us
    all_gather x1, waiting for transfers between devices, on_device(): hidden_all = lax.all_gather(hidden, 'blk', axis=1, tiled=True)  78 us
    all_to_all x1, blocking collectives, on_device(): lax.all_to_all(outgoing, 'expert', split_axis=0, concat_axis=0, tiled=True)  55.6 us
    all_gather x1, blocking collectives, on_device(): lax.all_gather(weighting.reshape(tok_dev, experts * CAP), 'blk', axis=0,...  34.7 us
    all_to_all x1, blocking collectives, on_device(): lax.all_to_all(partial_out, 'blk', split_axis=0, concat_axis=1, tiled=True)  20.2 us
    all_to_all x1, waiting for transfers between devices, on_device(): lax.all_to_all(slices, 'expert', split_axis=0, concat_axis=0, tiled=True)  9.16 us
    dot_general x1, matrix products, on_device(): jnp.dot(hidden_all, down_mat, preferred_element_type=jnp.float32)  9.07 us
    all_to_all x1, starting transfers between devices, on_device(): lax.all_to_all(slices, 'expert', split_axis=0, concat_axis=0, tiled=True)  8.62 us
  transfers between devices with their start and end apart: 2, of which 2 were waited for; matrix products, arithmetic and copies ran while one was open for 0% of the time, Pallas kernels for 0%

profile of v1, /device:TPU:8, one launch (start us, length us, event | category | flops | bytes accessed | tf_op | source)
XLA Modules:
  0.0 423.0 jit_solution(14849046578476247793)
XLA Ops:
  6.5 0.0 copy-start
  6.5 0.0 all-gather.2.cloned.1.call-start
  6.5 0.8 fusion.17
  7.3 0.1 copy.44
  7.4 0.1 reduce_window_sum.11
  7.6 0.1 copy.45
  7.7 0.1 copy-done
  7.7 0.6 convolution_convert_fusion
  8.4 1.4 copy.51
  9.8 55.6 %all_to_all.31 = bf16[32,4,7168]{2,1,0:T(4,128)(2,1)S(1)} all-to-all(bf16[32,4,7168]{2,1,0:T(4,128)(2,1)S(1)} %copy.51), channel_id=1, replica_groups=mesh['expert'=32,'blk'=8] {'expert'}, dimensions={0} | all-to-all | bytes 3670016 | tf_op jit(solution)/shard_map/all_to_all | solution.py:41
  65.4 1.5 stack_reshape.2
  66.9 3.7 stack.3
  70.6 0.0 copy-start.4
  70.6 168.8 %all_to_all.32 = bf16[8,128,7168]{2,1,0:T(8,128)(2,1)S(1)} all-to-all(bf16[8,128,7168]{2,1,0:T(8,128)(2,1)S(1)} %stack.3), channel_id=1, replica_groups=mesh['expert'=32,'blk'=8] {'blk'}, dimensions={0} | all-to-all | bytes 29360128 | tf_op jit(solution)/shard_map/all_to_all | solution.py:44
  239.5 0.0 copy-done.4
  239.5 0.0 copy-start.5
  239.5 3.9 fusion.4
  243.4 0.0 copy-done.5
  243.4 4.8 %fusion.12 = bf16[1024,256]{1,0:T(8,128)(2,1)} fusion(bf16[1024,7168]{1,0:T(8,128)(2,1)S(1)} %bitcast.39, bf16[1,7168,256]{2,1,0:T(8,128)(2,1)S(1)} %copy-done.5, f32[1024,256]{1,0:T(8,128)S(1)} %fusion.4), kind=kOutput, calls=%fused_computation.10 | convolution fusion | flops 3759669248 | bytes 19922944 | tf_op jit(solution)/shard_map/dot_general | solution.py:25
  248.2 0.0 all-gather.2.cloned.1.call-update
  248.2 78.0 %all-gather.2.cloned.1.call-done = bf16[1024,2048]{1,0:T(8,128)(2,1)} async-done(((bf16[1024,256]{1,0:T(8,128)(2,1)}), bf16[1024,2048]{1,0:T(8,128)(2,1)}) %all-gather.2.cloned.1.call-update) | async-done | bytes 4194320 | tf_op jit(solution)/shard_map/all_gather | solution.py:47
  326.2 9.1 %fusion.6 = bf16[1024,896]{1,0:T(8,128)(2,1)} fusion(bf16[1024,2048]{1,0:T(8,128)(2,1)} %all-gather.2.cloned.1.call-done, bf16[1,2048,896]{2,1,0:T(8,128)(2,1)} %param.11), kind=kOutput, calls=%fused_computation.8 | convolution fusion | flops 3759013888 | bytes 9699328 | tf_op jit(solution)/shard_map/dot_general | solution.py:48
  335.3 3.1 reshape.45
  338.4 0.3 copy.52
  338.7 0.0 copy-start.3
  338.7 0.0 copy-start.2
  338.7 1.8 copy.53
  340.6 8.6 %all-to-all-start.2 = ((bf16[32,32,896]{2,1,0:T(8,128)(2,1)}), bf16[32,32,896]{2,1,0:T(8,128)(2,1)S(1)}, u32[]{:S(2)}, u32[]{:S(2)}) async-start(bf16[32,32,896]{2,1,0:T(8,128)(2,1)} %copy.53), calls=%async_computation.2 | async-start | bytes 3670016 | tf_op jit(solution)/shard_map/all_to_all | solution.py:54
  349.2 0.1 copy.46
  349.3 0.1 copy.47
  349.4 0.0 copy-done.3
  349.4 0.0 copy-done.2
  349.5 0.1 copy.48
  349.6 0.1 eq.43
  349.7 34.7 %all_gather.6 = bf16[512,128]{1,0:T(8,128)(2,1)S(1)} all-gather(bf16[64,128]{1,0:T(8,128)(2,1)S(1)} %select_convert_fusion), channel_id=1, replica_groups=mesh['expert'=32,'blk'=8] {'blk'}, dimensions={0}, use_global_device_ids=true | all-gather | bytes 147456 | tf_op jit(solution)/shard_map/all_gather | solution.py:51
  384.4 0.1 copy.49
  384.5 0.2 reshape.43
  384.7 9.2 %all-to-all-done.2 = bf16[32,32,896]{2,1,0:T(8,128)(2,1)S(1)} async-done(((bf16[32,32,896]{2,1,0:T(8,128)(2,1)}), bf16[32,32,896]{2,1,0:T(8,128)(2,1)S(1)}, u32[]{:S(2)}, u32[]{:S(2)}) %all-to-all-start.2) | async-done | bytes 1835040 | tf_op jit(solution)/shard_map/all_to_all | solution.py:54
  393.9 0.0 copy-start.1
  393.9 0.6 copy.54
  394.4 0.5 bitcast_convert_fusion
  394.9 20.2 %all_to_all.33 = bf16[8,64,896]{2,1,0:T(8,128)(2,1)S(1)} all-to-all(bf16[8,64,896]{2,1,0:T(8,128)(2,1)S(1)} %bitcast_convert_fusion), channel_id=1, replica_groups=mesh['expert'=32,'blk'=8] {'blk'}, dimensions={0} | all-to-all | bytes 1835008 | tf_op jit(solution)/shard_map/all_to_all | solution.py:60
  415.1 1.1 copy.58
  416.2 0.0 copy-done.1
  (10 shorter events, 0.2 us)
Async XLA Ops:
  6.5 1.2 copy-start
  6.5 319.7 %all-gather.2.cloned.1.call-start = ((), (), s32[]{:S(2)}) async-start(), calls=%async_computation.4 | async-start | bytes 4718592 | tf_op jit(solution)/shard_map/all_gather | solution.py:47
  70.6 168.8 %copy-start.4 = (bf16[1,7168,256]{2,1,0:T(8,128)(2,1)S(1)}, bf16[1,7168,256]{2,1,0:T(8,128)(2,1)}, u32[]{:S(2)}) copy-start(bf16[1,7168,256]{2,1,0:T(8,128)(2,1)} %param.9) | copy-start | bytes 11010052
  239.5 4.0 copy-start.5
  338.7 10.7 %copy-start.3 = (bf16[64,8]{0,1:T(8,128)(2,1)S(1)}, bf16[64,8]{0,1:T(8,128)(2,1)}, u32[]{:S(2)}) copy-start(bf16[64,8]{0,1:T(8,128)(2,1)} %param.8) | copy-start | bytes 3076
  338.7 10.7 %copy-start.2 = (s32[64,8]{0,1:T(8,128)S(1)}, s32[64,8]{0,1:T(8,128)}, u32[]{:S(2)}) copy-start(s32[64,8]{0,1:T(8,128)} %param.7) | copy-start | bytes 6148
  340.6 53.3 %all-to-all-start.2 = ((bf16[32,32,896]{2,1,0:T(8,128)(2,1)}), bf16[32,32,896]{2,1,0:T(8,128)(2,1)S(1)}, u32[]{:S(2)}, u32[]{:S(2)}) async-start(bf16[32,32,896]{2,1,0:T(8,128)(2,1)} %copy.53), calls=%async_computation.2 | async-start | bytes 3670016 | tf_op jit(solution)/shard_map/all_to_all | solution.py:54
  393.9 22.3 %copy-start.1 = (bf16[64,7168]{1,0:T(8,128)(2,1)S(1)}, bf16[64,7168]{1,0:T(8,128)(2,1)}, u32[]{:S(2)}) copy-start(bf16[64,7168]{1,0:T(8,128)(2,1)} %param.6) | copy-start | bytes 2752516
Sparse Core Ops, SparseCore 0:
  248.3 77.8 all-gather.1
